TPU v7x, 256 devices: a whole 4x4x8 slice. The times are simulated.
256 devices in a mesh: ctx: 64 (over y, z, x_hi), tp: 4 (over x_lo, core).
Axes of the slice: x: 4 (x_hi: 2, x_lo: 2; x = x_hi * 2 + x_lo), y: 4, z: 8, core: 2. Of those that a mesh axis runs over, the one named last changes fastest.
Arguments:
- queries: bfloat16 [4096, 3584], P('ctx', 'tp'), may hold values from -6 to 6
- keys: bfloat16 [4096, 512], P('ctx', 'tp'), may hold values from -5 to 5
- values: bfloat16 [4096, 512], P('ctx', 'tp'), may hold values from -6 to 6
- block_table: int32 [64], replicated, may hold values from 0 to 63, each once
- residual: bfloat16 [4096, 3584], P(('ctx', 'tp')), may hold values from -6 to 6
- out_weight: bfloat16 [3584, 3584], P('tp'), may hold values from -0.5 to 0.5
- norm_gain: bfloat16 [3584], replicated, may hold values from 0.099609375 to 1.8984375
- gate_logit_weight: bfloat16 [3584], replicated, may hold values from -0.09375 to 0.09375
- gate_weight: bfloat16 [3584, 20480], P(None, 'ctx'), may hold values from -0.09375 to 0.09375
- up_weight: bfloat16 [3584, 20480], P(None, 'ctx'), may hold values from -0.09375 to 0.09375
- down_weight: bfloat16 [20480, 3584], P('ctx'), may hold values from -0.0390625 to 0.0390625
Outputs:
- layer_out: bfloat16 [4096, 3584], P(('ctx', 'tp'))
Inputs may be any that keep to these rules, and one draw needn't show every extreme that they name: Each entry names a different pair; slot c holds blocks block_table[c] and its mirror, counted from the end of the prompt.
All inputs are finite; a program needn't handle non-finite values.
Results may differ from a plain program's by a relative error of at most 0.017.
Values may be sent and summed in bfloat16 or wider, within the bound.
No kernel may reach another device: no remote copies, remote signals or barrier semaphores. Data moves between devices by JAX's collectives and lax.ppermute only.
A program may use at most 128 MiB of HBM per device.

v0:
```python
import jax
import jax.numpy as jnp
from jax import lax
from jax.sharding import PartitionSpec as P

HEADS = 28
KV_HEADS = 4
HEAD_DIM = 128


def per_device(
    queries,
    keys,
    values,
    block_table,
    residual,
    out_weight,
    norm_gain,
    gate_logit_weight,
    gate_weight,
    up_weight,
    down_weight,
):
    tokens = queries.shape[0]
    half = tokens // 2
    ctx_count = lax.axis_size("ctx")
    tp_count = lax.axis_size("tp")
    quarter = tokens // tp_count
    group = HEADS // KV_HEADS
    kv_local = keys.shape[1] // HEAD_DIM
    scale = HEAD_DIM ** (-0.5)
    mirror = 2 * ctx_count - 1
    slots = jnp.arange(ctx_count, dtype=jnp.int32)

    def row_positions(first_row, count):
        rows = first_row + jnp.arange(count, dtype=jnp.int32)
        owner = rows // tokens
        local = rows % tokens
        onehot = (owner[:, None] == slots[None, :]).astype(jnp.int32)
        pair = jnp.sum(onehot * block_table[None, :], axis=1)
        return jnp.where(local < half, pair * half + local, (mirror - pair) * half + local - half)

    own_place = row_positions(lax.axis_index("ctx") * tokens, tokens)
    query_heads = queries.reshape(tokens, kv_local, group, HEAD_DIM)
    start_max = jnp.full((kv_local, group, tokens), -1e30, jnp.float32)
    key_piece = lax.all_gather(keys, "ctx", axis=0, tiled=True)
    value_piece = lax.all_gather(values, "ctx", axis=0, tiled=True)
    count = key_piece.shape[0]
    key_place = row_positions(jnp.int32(0), count)
    key_heads = key_piece.reshape(count, kv_local, HEAD_DIM)
    value_heads = value_piece.reshape(count, kv_local, HEAD_DIM)
    score = (
        jnp.einsum("tkgd,pkd->kgtp", query_heads, key_heads, preferred_element_type=jnp.float32)
        * scale
    )
    visible = key_place[None, :] <= own_place[:, None]
    score = jnp.where(visible, score, -1e30)
    new_max = jnp.maximum(start_max, jnp.max(score, axis=-1))
    weight = jnp.where(visible, jnp.exp(score - new_max[..., None]), 0.0)
    new_sum = jnp.sum(weight, axis=-1)
    added = jnp.einsum(
        "kgtp,pkd->kgtd",
        weight.astype(jnp.bfloat16),
        value_heads,
        preferred_element_type=jnp.float32,
    )
    summed = added / new_sum[..., None]
    attended_heads = (
        jnp.transpose(summed, (2, 0, 1, 3))
        .astype(jnp.bfloat16)
        .reshape(tokens, kv_local * group * HEAD_DIM)
    )
    projected = jnp.dot(attended_heads, out_weight, preferred_element_type=jnp.float32)
    total = lax.psum(projected.astype(jnp.bfloat16), "tp").astype(jnp.float32)
    head_sum = lax.dynamic_slice_in_dim(total, lax.axis_index("tp") * quarter, quarter, 0)
    attended = (residual.astype(jnp.float32) + head_sum).astype(jnp.bfloat16)
    attended = lax.optimization_barrier(attended)
    attended_f = attended.astype(jnp.float32)
    mean_square = jnp.mean(attended_f * attended_f, axis=-1, keepdims=True)
    normed = (attended_f * lax.rsqrt(mean_square + 1e-06) * norm_gain.astype(jnp.float32)).astype(
        jnp.bfloat16
    )
    gate_prob = jax.nn.sigmoid(
        jnp.dot(normed, gate_logit_weight, preferred_element_type=jnp.float32)
    )
    piece = lax.all_gather(normed, "ctx", axis=0, tiled=True)
    gate_part = jnp.dot(piece, gate_weight, preferred_element_type=jnp.float32)
    up_part = jnp.dot(piece, up_weight, preferred_element_type=jnp.float32)
    hidden = (jax.nn.silu(gate_part) * up_part).astype(jnp.bfloat16)
    rows = hidden
    shared = lax.psum_scatter(
        jnp.dot(rows, down_weight, preferred_element_type=jnp.float32),
        "ctx",
        scatter_dimension=0,
        tiled=True,
    )
    return (attended_f + gate_prob[:, None] * shared).astype(jnp.bfloat16)


def solution(mesh):
    return jax.shard_map(
        per_device,
        mesh=mesh,
        in_specs=(
            P("ctx", "tp"),
            P("ctx", "tp"),
            P("ctx", "tp"),
            P(),
            P(("ctx", "tp"), None),
            P("tp", None),
            P(),
            P(),
            P(None, "ctx"),
            P(None, "ctx"),
            P("ctx", None),
        ),
        out_specs=P(("ctx", "tp"), None),
        check_vma=False,
    )
```

profile of v0, /device:TPU:0, one launch (start us, length us, event | category | flops | bytes accessed | tf_op | source)
XLA Modules:
  0.0 864.5 jit_solution(11348240395880294920)
XLA Ops:
  6.5 0.7 all-gather.4.cloned.1.call-update
  7.3 0.0 all-gather.6.cloned.1.call-start
  7.3 0.7 all-gather.6.cloned.1.call-update
  8.0 0.0 all-reduce.2.cloned.1.call-start
  8.1 0.8 select_reduce_fusion.1
  8.9 0.9 select_reduce_fusion
  9.9 0.2 broadcast_compare_fusion
  10.1 116.2 %all-gather.4.cloned.1.call-done = bf16[4096,128]{1,0:T(8,128)(2,1)} async-done(((bf16[64,128]{1,0:T(8,128)(2,1)}), bf16[4096,128]{1,0:T(8,128)(2,1)}) %all-gather.4.cloned.1.call-update) | async-done | bytes 1048592 | tf_op jit(solution)/shard_map/all_gather | solution.py:46
  126.3 2.7 fusion
  129.0 2.9 copy-done.1
  131.9 2.2 fusion.1
  134.1 106.7 %all-gather.6.cloned.1.call-done = bf16[4096,128]{1,0:T(8,128)(2,1)} async-done(((bf16[64,128]{1,0:T(8,128)(2,1)}), bf16[4096,128]{1,0:T(8,128)(2,1)}) %all-gather.6.cloned.1.call-update) | async-done | bytes 1048592 | tf_op jit(solution)/shard_map/all_gather | solution.py:47
  240.9 5.2 fusion.19
  246.1 0.1 copy.16
  246.1 4.8 convolution_convert_fusion
  251.0 0.0 all-reduce.2.cloned.1.call-update
  251.0 0.0 all-gather.8.cloned.1.call-start
  251.1 39.2 %all-reduce.2.cloned.1.call-done = bf16[64,3584]{1,0:T(8,128)(2,1)} async-done(((bf16[64,3584]{1,0:T(8,128)(2,1)}), bf16[64,3584]{1,0:T(8,128)(2,1)}) %all-reduce.2.cloned.1.call-update) | async-done | bytes 458768 | tf_op jit(solution)/shard_map/psum | solution.py:74
  290.3 0.9 add_convert_fusion
  291.3 0.1 fusion.26
  291.4 0.7 fusion.28
  292.2 0.0 all-gather.8.cloned.1.call-update
  292.2 0.2 reduce-scatter.2.cloned.1.call-start
  292.4 147.2 %all-gather.8.cloned.1.call-done = bf16[1024,3584]{1,0:T(8,128)(2,1)} async-done(((bf16[16,3584]{1,0:T(8,128)(2,1)}), bf16[1024,3584]{1,0:T(8,128)(2,1)}) %all-gather.8.cloned.1.call-update) | async-done | bytes 7340048 | tf_op jit(solution)/shard_map/all_gather | solution.py:86
  439.7 7.4 fusion.44
  447.1 12.9 %fusion.8 = f32[1024,3584]{1,0:T(8,128)} fusion(bf16[320,3584]{1,0:T(8,128)(2,1)S(1)} %copy-done, bf16[1024,3584]{1,0:T(8,128)(2,1)} %all-gather.8.cloned.1.call-done, bf16[3584,320]{0,1:T(8,128)(2,1)} %param.20, f32[1024,320]{0,1:T(8,128)} %fusion.44), kind=kOutput, calls=%fused_computation.11 | convolution fusion | flops 4699586560 | bytes 27918336 | tf_op jit(solution)/shard_map/dot_general | solution.py:92
  460.0 0.0 reduce-scatter.2.cloned.1.call-update
  460.0 0.7 copy-done.5
  460.7 0.2 copy-done.2
  460.9 0.1 fusion.12
  461.1 395.3 %reduce-scatter.2.cloned.1.call-done = f32[16,3584]{1,0:T(8,128)} async-done(((f32[1024,3584]{1,0:T(8,128)}), f32[16,3584]{1,0:T(8,128)}) %reduce-scatter.2.cloned.1.call-update) | async-done | bytes 229392 | tf_op jit(solution)/shard_map/reduce_scatter | solution.py:91
  856.3 1.7 fusion.29
  (18 shorter events, 0.1 us)
Async XLA Ops:
  6.5 440.5 %copy-start = (bf16[320,3584]{1,0:T(8,128)(2,1)S(1)}, bf16[320,3584]{1,0:T(8,128)(2,1)}, u32[]{:S(2)}) copy-start(bf16[320,3584]{1,0:T(8,128)(2,1)} %param.21) | copy-start | bytes 6881284
  6.5 119.8 %all-gather.4.cloned.1.call-start = ((), (), s32[]{:S(2)}) async-start(), calls=%async_computation.1 | async-start | bytes 1064960 | tf_op jit(solution)/shard_map/all_gather | solution.py:46
  7.3 233.6 %all-gather.6.cloned.1.call-start = ((), (), s32[]{:S(2)}) async-start(), calls=%async_computation.2 | async-start | bytes 1064960 | tf_op jit(solution)/shard_map/all_gather | solution.py:47
  8.0 282.3 %all-reduce.2.cloned.1.call-start = ((), (), s32[]{:S(2)}) async-start(), calls=%async_computation.3 | async-start | bytes 917504 | tf_op jit(solution)/shard_map/psum | solution.py:74
  129.0 3.0 copy-start.1
  246.0 5.0 copy-start.4
  246.0 44.3 %copy-start.3 = (bf16[16,3584]{1,0:T(8,128)(2,1)S(1)}, bf16[16,3584]{1,0:T(8,128)(2,1)}, u32[]{:S(2)}) copy-start(bf16[16,3584]{1,0:T(8,128)(2,1)} %param.15) | copy-start | bytes 344068
  251.0 188.6 %all-gather.8.cloned.1.call-start = ((), (), s32[]{:S(2)}) async-start(), calls=%async_computation.4 | async-start | bytes 7454720 | tf_op jit(solution)/shard_map/all_gather | solution.py:86
  292.2 564.1 %reduce-scatter.2.cloned.1.call-start = ((), (), s32[]{:S(2)}) async-start(), calls=%async_computation.5 | async-start | bytes 14909440 | tf_op jit(solution)/shard_map/reduce_scatter | solution.py:91
  460.0 0.7 copy-start.5
  460.0 0.9 copy-start.2
Sparse Core Ops, SparseCore 0:
  10.9 115.3 all-gather.3
  129.8 111.0 all-gather.5
  251.1 39.1 all-reduce.1
  294.2 145.3 all-gather.7
  460.1 396.1 reduce-scatter.1
where the time goes:
time: 865 us
  waiting for transfers between devices  806 us (93%)
  matrix products  33.1 us (4%)
  between operations  13.3 us (2%)
    reduce_scatter x1, waiting for transfers between devices, per_device(): lax.psum_scatter(jnp.dot(rows, down_weight, preferred_element_type=jnp.fl...  395 us
    all_gather x1, waiting for transfers between devices, per_device(): piece = lax.all_gather(normed, 'ctx', axis=0, tiled=True)  147 us
    all_gather x1, waiting for transfers between devices, per_device(): key_piece = lax.all_gather(keys, 'ctx', axis=0, tiled=True)  116 us
    all_gather x1, waiting for transfers between devices, per_device(): value_piece = lax.all_gather(values, 'ctx', axis=0, tiled=True)  107 us
    psum x1, waiting for transfers between devices, per_device(): total = lax.psum(projected.astype(jnp.bfloat16), 'tp').astype(jnp.float32)  39.2 us
  transfers between devices with their start and end apart: 5, of which 5 were waited for; matrix products, arithmetic and copies ran while one was open for 1% of the time, Pallas kernels for 0%

commit v1 on v0

--- a/solution.py
+++ b/solution.py
@@ -83,7 +83,9 @@
     gate_prob = jax.nn.sigmoid(
         jnp.dot(normed, gate_logit_weight, preferred_element_type=jnp.float32)
     )
-    piece = lax.all_gather(normed, "ctx", axis=0, tiled=True)
+    piece = jnp.concatenate(
+        lax.all_to_all(jnp.stack([normed] * lax.axis_size("ctx")), "ctx", 0, 0), axis=0
+    )
     gate_part = jnp.dot(piece, gate_weight, preferred_element_type=jnp.float32)
     up_part = jnp.dot(piece, up_weight, preferred_element_type=jnp.float32)
     hidden = (jax.nn.silu(gate_part) * up_part).astype(jnp.bfloat16)

time: 865 us -> 893 us (1.032)
  blocking collectives: 0 us -> 178 us
  waiting for transfers between devices: 806 us -> 655 us
    all_to_all x0 -> x1, blocking collectives: none -> 178 us  [per_device(): lax.all_to_all(jnp.stack([normed] * lax.axis_size('ctx')), 'ctx', 0, 0)]
    all_gather x1 -> x0, waiting for transfers between devices: 147 us -> none  [per_device(): piece = lax.all_gather(normed, 'ctx', axis=0, tiled=True)]
  transfers between devices with their start and end apart: 5 -> 4, of which waited for: 5 -> 4; matrix products, arithmetic and copies ran while one was open for 1% -> 1% of each run, Pallas kernels for 0% -> 0%
where the time goes in v1:
time: 893 us; the launch traced here: 891 us
  waiting for transfers between devices  655 us (73%)
  blocking collectives  178 us (20%)
  matrix products  29.4 us (3%)
  between operations  13.3 us (1%)
    reduce_scatter x1, waiting for transfers between devices, per_device(): lax.psum_scatter(jnp.dot(rows, down_weight, preferred_element_type=jnp.fl...  391 us
    all_to_all x1, blocking collectives, per_device(): lax.all_to_all(jnp.stack([normed] * lax.axis_size('ctx')), 'ctx', 0, 0)  178 us
    all_gather x1, waiting for transfers between devices, per_device(): key_piece = lax.all_gather(keys, 'ctx', axis=0, tiled=True)  116 us
    all_gather x1, waiting for transfers between devices, per_device(): value_piece = lax.all_gather(values, 'ctx', axis=0, tiled=True)  107 us
    psum x1, waiting for transfers between devices, per_device(): total = lax.psum(projected.astype(jnp.bfloat16), 'tp').astype(jnp.float32)  39.2 us
  transfers between devices with their start and end apart: 4, of which 4 were waited for; matrix products, arithmetic and copies ran while one was open for 1% of the time, Pallas kernels for 0%

profile of v1, /device:TPU:0, one launch (start us, length us, event | category | flops | bytes accessed | tf_op | source)
XLA Modules:
  0.0 890.7 jit_solution(18384159389226386558)
XLA Ops:
  6.5 0.7 all-gather.3.cloned.1.call-update
  7.3 0.0 all-gather.5.cloned.1.call-start
  7.3 0.7 all-gather.5.cloned.1.call-update
  8.0 0.0 all-reduce.2.cloned.1.call-start
  8.1 0.8 select_reduce_fusion.1
  8.9 0.9 select_reduce_fusion
  9.9 0.2 broadcast_compare_fusion
  10.1 116.2 %all-gather.3.cloned.1.call-done = bf16[4096,128]{1,0:T(8,128)(2,1)} async-done(((bf16[64,128]{1,0:T(8,128)(2,1)}), bf16[4096,128]{1,0:T(8,128)(2,1)}) %all-gather.3.cloned.1.call-update) | async-done | bytes 1048592 | tf_op jit(solution)/shard_map/all_gather | solution.py:46
  126.3 2.7 fusion
  129.0 3.0 copy-done.2
  131.9 2.2 fusion.1
  134.1 106.7 %all-gather.5.cloned.1.call-done = bf16[4096,128]{1,0:T(8,128)(2,1)} async-done(((bf16[64,128]{1,0:T(8,128)(2,1)}), bf16[4096,128]{1,0:T(8,128)(2,1)}) %all-gather.5.cloned.1.call-update) | async-done | bytes 1048592 | tf_op jit(solution)/shard_map/all_gather | solution.py:47
  240.9 5.2 fusion.19
  246.0 0.0 copy-start.4
  246.1 0.1 copy.16
  246.1 4.9 convolution_convert_fusion
  251.0 0.0 all-reduce.2.cloned.1.call-update
  251.0 0.0 reduce-scatter.2.cloned.1.call-start
  251.1 39.2 %all-reduce.2.cloned.1.call-done = bf16[64,3584]{1,0:T(8,128)(2,1)} async-done(((bf16[64,3584]{1,0:T(8,128)(2,1)}), bf16[64,3584]{1,0:T(8,128)(2,1)}) %all-reduce.2.cloned.1.call-update) | async-done | bytes 458768 | tf_op jit(solution)/shard_map/psum | solution.py:74
  290.3 0.9 add_convert_fusion
  291.3 0.1 fusion.26
  291.4 0.1 fusion.28
  291.5 0.9 stack.2
  292.4 178.4 %all_to_all.5 = bf16[64,16,3584]{2,1,0:T(8,128)(2,1)S(1)} all-to-all(bf16[64,16,3584]{2,1,0:T(8,128)(2,1)S(1)} %stack.2), channel_id=1, replica_groups=mesh['ctx'=64,'tp'=4] {'ctx'}, dimensions={0} | all-to-all | bytes 14680064 | tf_op jit(solution)/shard_map/all_to_all | solution.py:87
  470.8 2.9 copy-done.1
  473.7 3.7 fusion.44
  477.4 12.9 %fusion.8 = f32[1024,3584]{1,0:T(8,128)} fusion(bf16[320,3584]{1,0:T(8,128)(2,1)S(1)} %copy-done, bf16[1024,3584]{1,0:T(8,128)(2,1)} %bitcast.77, bf16[3584,320]{0,1:T(8,128)(2,1)} %param.20, f32[1024,320]{0,1:T(8,128)} %fusion.44), kind=kOutput, calls=%fused_computation.11 | convolution fusion | flops 4699586560 | bytes 27918336 | tf_op jit(solution)/shard_map/dot_general | solution.py:94
  490.3 0.0 reduce-scatter.2.cloned.1.call-update
  490.4 0.7 copy-done.5
  491.0 0.1 fusion.12
  491.2 391.3 %reduce-scatter.2.cloned.1.call-done = f32[16,3584]{1,0:T(8,128)} async-done(((f32[1024,3584]{1,0:T(8,128)}), f32[16,3584]{1,0:T(8,128)}) %reduce-scatter.2.cloned.1.call-update) | async-done | bytes 229392 | tf_op jit(solution)/shard_map/reduce_scatter | solution.py:93
  882.5 1.7 fusion.29
  (19 shorter events, 0.1 us)
Async XLA Ops:
  6.5 470.9 %copy-start = (bf16[320,3584]{1,0:T(8,128)(2,1)S(1)}, bf16[320,3584]{1,0:T(8,128)(2,1)}, u32[]{:S(2)}) copy-start(bf16[320,3584]{1,0:T(8,128)(2,1)} %param.21) | copy-start | bytes 6881284
  6.5 119.8 %all-gather.3.cloned.1.call-start = ((), (), s32[]{:S(2)}) async-start(), calls=%async_computation.2 | async-start | bytes 1064960 | tf_op jit(solution)/shard_map/all_gather | solution.py:46
  7.3 233.6 %all-gather.5.cloned.1.call-start = ((), (), s32[]{:S(2)}) async-start(), calls=%async_computation.3 | async-start | bytes 1064960 | tf_op jit(solution)/shard_map/all_gather | solution.py:47
  8.0 282.3 %all-reduce.2.cloned.1.call-start = ((), (), s32[]{:S(2)}) async-start(), calls=%async_computation.4 | async-start | bytes 917504 | tf_op jit(solution)/shard_map/psum | solution.py:74
  129.0 3.0 copy-start.2
  246.0 5.0 copy-start.4
  246.0 44.3 %copy-start.3 = (bf16[16,3584]{1,0:T(8,128)(2,1)S(1)}, bf16[16,3584]{1,0:T(8,128)(2,1)}, u32[]{:S(2)}) copy-start(bf16[16,3584]{1,0:T(8,128)(2,1)} %param.15) | copy-start | bytes 344068
  251.0 631.5 %reduce-scatter.2.cloned.1.call-start = ((), (), s32[]{:S(2)}) async-start(), calls=%async_computation.5 | async-start | bytes 14909440 | tf_op jit(solution)/shard_map/reduce_scatter | solution.py:93
  292.4 181.3 %copy-start.6 = (bf16[3584,320]{0,1:T(8,128)(2,1)S(1)}, bf16[3584,320]{0,1:T(8,128)(2,1)}, u32[]{:S(2)}) copy-start(bf16[3584,320]{0,1:T(8,128)(2,1)} %param.19) | copy-start | bytes 6881284
  470.8 2.9 copy-start.1
  490.3 0.7 copy-start.5
Sparse Core Ops, SparseCore 0:
  10.9 115.3 all-gather.2
  129.8 111.0 all-gather.4
  251.1 39.1 all-reduce.1
  490.5 391.9 reduce-scatter.1
